TPU v7x, 128 devices: a whole 4x4x4 slice. The times are simulated.
128 devices in a mesh: ctx: 32 (over x, y, core), heads: 4 (over z).
Axes of the slice: x: 4, y: 4, z: 4, core: 2. Of those that a mesh axis runs over, the one named last changes fastest.
Arguments:
- queries: bfloat16 [32, 32768, 128], P('heads', 'ctx'), may hold values from -6 to 6
- keys: bfloat16 [32, 32768, 128], P('heads', 'ctx'), may hold values from -6 to 6
- values: bfloat16 [32, 32768, 128], P('heads', 'ctx'), may hold values from -6 to 6
- out_grad: bfloat16 [32, 32768, 128], P('heads', 'ctx'), may hold values from -6 to 6
- level_table: float32 [64, 16], replicated, may hold values from 0.2 to 2
- table_index: int32 [32768], P('ctx'), may hold values from 0 to 63
Outputs:
- attention_out: bfloat16 [32, 32768, 128], P('heads', 'ctx')
- query_grad: bfloat16 [32, 32768, 128], P('heads', 'ctx')
- key_grad: bfloat16 [32, 32768, 128], P('heads', 'ctx')
- value_grad: bfloat16 [32, 32768, 128], P('heads', 'ctx')
- table_grad: float32 [64, 16], replicated
All inputs are finite; a program needn't handle non-finite values.
Results may differ from a plain program's by a relative error of at most 0.0058.
Values sent between devices are 32-bit elements; how exact they have to be, the bound alone decides.
A program may use at most 256 MiB of HBM per device.

v0:
```python
import math
import jax
import jax.numpy as jnp
from jax import lax
from jax.sharding import PartitionSpec as P


def level_grid(length):
    row_ids = lax.broadcasted_iota(jnp.int32, (length, length), 0)
    col_ids = lax.broadcasted_iota(jnp.int32, (length, length), 1)
    crossed = jnp.bitwise_xor(row_ids, col_ids)
    levels = jnp.zeros((length, length), jnp.int32)
    for bit_pos in range(length.bit_length()):
        levels = levels + (crossed >= 1 << bit_pos).astype(jnp.int32)
    return (levels, col_ids <= row_ids)


def lookup(level_table, table_index):
    matches = table_index[:, None] == jnp.arange(level_table.shape[0], dtype=jnp.int32)[None, :]
    lam_all = jnp.sum(jnp.where(matches[:, :, None], level_table[None], 0.0), 1)
    return (matches, lam_all)


def block_start(queries, keys, values, out_grad, lam_tok, block_id, level_bits, factor):
    first_cross = queries.shape[1].bit_length()
    states = jnp.einsum("htd,hte->hde", keys, values, preferred_element_type=jnp.float32)
    pieces = []
    for bit_num in range(level_bits):
        scaled = (lam_tok[:, first_cross + bit_num][None, :, None] * out_grad).astype(jnp.bfloat16)
        upper_half = jnp.right_shift(block_id, bit_num) & 1 == 1
        bucket_grad = factor * jnp.einsum(
            "htd,hte->hde", queries, scaled, preferred_element_type=jnp.float32
        )
        pieces.append(jnp.where(upper_half, bucket_grad, jnp.zeros_like(bucket_grad)))
    return (states, jnp.stack(pieces))


def block_finish(queries, keys, values, out_grad, lam_tok, bucket, state_grad, factor):
    length = queries.shape[1]
    level_bits = bucket.shape[0]
    first_cross = length.bit_length()
    levels, causal = level_grid(length)
    weight = jnp.zeros((length, length), jnp.float32)
    for level_id in range(first_cross):
        weight = weight + jnp.where(levels == level_id, lam_tok[:, level_id : level_id + 1], 0.0)
    weight = factor * jnp.where(causal, weight, 0.0)
    dot_scores = jnp.einsum("htd,hsd->hts", queries, keys, preferred_element_type=jnp.float32)
    weighted = (weight[None] * dot_scores).astype(jnp.bfloat16)
    out_local = jnp.einsum("hts,hsd->htd", weighted, values, preferred_element_type=jnp.float32)
    grad_weighted = jnp.einsum("htd,hsd->hts", out_grad, values, preferred_element_type=jnp.float32)
    grad_scores = (weight[None] * grad_weighted).astype(jnp.bfloat16)
    query_local = jnp.einsum("hts,hsd->htd", grad_scores, keys, preferred_element_type=jnp.float32)
    key_local = jnp.einsum("hts,htd->hsd", grad_scores, queries, preferred_element_type=jnp.float32)
    value_local = jnp.einsum("hts,htd->hsd", weighted, out_grad, preferred_element_type=jnp.float32)
    weight_grad = jnp.sum(dot_scores * grad_weighted, 0)
    lam_cross = lam_tok[:, first_cross : first_cross + level_bits].T[:, None, :, None]
    cross = jnp.einsum("htd,jhde->jhte", queries, bucket, preferred_element_type=jnp.float32)
    attention_out = out_local + factor * jnp.sum(lam_cross * cross, 0)
    back_cross = jnp.einsum("hte,jhde->jhtd", out_grad, bucket, preferred_element_type=jnp.float32)
    query_grad = query_local + factor * jnp.sum(lam_cross * back_cross, 0)
    key_grad = key_local + jnp.einsum(
        "hte,hde->htd", values, state_grad, preferred_element_type=jnp.float32
    )
    value_grad = value_local + jnp.einsum(
        "htd,hde->hte", keys, state_grad, preferred_element_type=jnp.float32
    )
    local_cols = [
        factor * jnp.sum(jnp.where(causal & (levels == level_id), weight_grad, 0.0), 1)
        for level_id in range(first_cross)
    ]
    lam_local = jnp.stack(local_cols, 1)
    lam_far = factor * jnp.sum(cross * out_grad.astype(jnp.float32)[None], axis=(1, 3))
    spare = jnp.zeros((length, lam_tok.shape[1] - first_cross - level_bits), jnp.float32)
    lam_grad = jnp.concatenate([lam_local, lam_far.T, spare], 1)
    return (
        attention_out.astype(jnp.bfloat16),
        query_grad.astype(jnp.bfloat16),
        key_grad.astype(jnp.bfloat16),
        value_grad.astype(jnp.bfloat16),
        lam_grad,
    )


def in_bucket(owners, block_id, bit_num):
    same_top = jnp.right_shift(owners, bit_num + 1) == jnp.right_shift(block_id, bit_num + 1)
    owner_low = jnp.right_shift(owners, bit_num) & 1 == 0
    mine_high = jnp.right_shift(block_id, bit_num) & 1 == 1
    return same_top & owner_low & mine_high


def body(queries, keys, values, out_grad, level_table, table_index):
    head_local, length, head_width = queries.shape
    devices = lax.axis_size("ctx")
    level_bits = devices.bit_length() - 1
    factor = 1.0 / math.sqrt(head_width * length * devices)
    block_id = lax.axis_index("ctx")
    matches, lam_tok = lookup(level_table, table_index)
    states, grads = block_start(
        queries, keys, values, out_grad, lam_tok, block_id, level_bits, factor
    )
    shard_piece = lax.all_gather(states[None], "ctx", axis=0, tiled=True)
    owners = jnp.arange(shard_piece.shape[0], dtype=jnp.int32)
    pieces = []
    for bit_num in range(level_bits):
        member = in_bucket(owners, block_id, bit_num)
        pieces.append(jnp.sum(jnp.where(member[:, None, None, None], shard_piece, 0.0), 0))
    bucket = jnp.stack(pieces)
    bucket = bucket.astype(jnp.bfloat16)
    row_total = head_local * lax.axis_size("ctx")
    owners = jnp.arange(row_total // head_local, dtype=jnp.int32)
    term = jnp.zeros((row_total // head_local,) + states.shape, jnp.float32)
    for bit_num in range(level_bits):
        member = in_bucket(owners, block_id, bit_num)
        term = term + jnp.where(member[:, None, None, None], grads[bit_num][None], 0.0)
    state_grad = lax.psum_scatter(
        term.reshape((row_total,) + states.shape[1:]), "ctx", scatter_dimension=0, tiled=True
    )
    state_grad = state_grad.astype(jnp.bfloat16)
    attention_out, query_grad, key_grad, value_grad, lam_grad = block_finish(
        queries, keys, values, out_grad, lam_tok, bucket, state_grad, factor
    )
    table_part = jnp.sum(jnp.where(matches[:, :, None], lam_grad[:, None, :], 0.0), 0)
    table_total = lax.psum(table_part, ("ctx", "heads"))
    table_grad = table_total / math.sqrt(length * devices)
    return (attention_out, query_grad, key_grad, value_grad, table_grad)


def solution(mesh):
    placed = (
        P("heads", "ctx", None),
        P("heads", "ctx", None),
        P("heads", "ctx", None),
        P("heads", "ctx", None),
        P(),
        P("ctx"),
    )
    return jax.shard_map(
        body,
        mesh=mesh,
        in_specs=placed,
        out_specs=(
            P("heads", "ctx", None),
            P("heads", "ctx", None),
            P("heads", "ctx", None),
            P("heads", "ctx", None),
            P(),
        ),
        check_vma=False,
    )
```

profile of v0, /device:TPU:1, one launch (start us, length us, event | category | flops | bytes accessed | tf_op | source)
XLA Modules:
  0.0 370.0 jit_solution(8418169630844257545)
XLA Ops:
  7.2 0.0 copy-start
  7.2 0.0 reduce-scatter.2.cloned.1.call-start
  7.3 0.1 broadcast_in_dim.340
  7.3 0.1 broadcast_in_dim.341
  7.4 0.1 broadcast_in_dim.335
  7.5 0.1 broadcast_in_dim.336
  7.6 0.1 broadcast_in_dim.350
  7.7 0.1 broadcast_in_dim.351
  7.8 0.1 broadcast_in_dim.345
  7.9 0.1 broadcast_in_dim.346
  8.0 0.1 broadcast_in_dim.329
  8.1 0.1 broadcast_in_dim.330
  8.2 0.8 copy.72
  9.0 0.9 iota_compare_fusion.1
  9.8 0.0 copy-start.7
  9.9 0.6 copy-done.7
  10.5 0.5 select_reduce_fusion.17
  11.1 0.0 copy-done
  11.1 2.6 fusion.100
  13.7 0.0 copy-done.3
  13.7 1.1 fusion.64
  14.9 1.1 fusion.91
  16.0 1.1 fusion.82
  17.1 1.1 fusion.73
  18.3 8.7 %fusion.2 = f32[256,128,128]{1,2,0:T(8,128)} fusion(f32[8,128,128]{1,2,0:T(8,128)S(1)} %fusion.100, f32[8,128,128]{1,2,0:T(8,128)S(1)} %fusion.91, f32[8,128,128]{1,2,0:T(8,128)S(1)} %fusion.82, f32[8,128,128]{1,2,0:T(8,128)S(1)} %fusion.73, f32[8,128,128]{1,2,0:T(8,128)S(1)} %fusion.64, pred[256]{0:T(512)(128)(4,1)S(1)} %broadcast_in_dim.351, ...), kind=kLoop, calls=%fused_computation.9 | loop fusion | flops 37748736 | bytes 19399936 | tf_op jit(solution)/shard_map/add | solution.py:114
  27.0 0.0 reduce-scatter.2.cloned.1.call-update
  27.0 0.2 all-gather.3.cloned.1.call-start
  27.2 3.8 %fusion.106 = f32[8,128,128]{2,1,0:T(8,128)} fusion(bf16[8,1024,128]{2,1,0:T(8,128)(2,1)} %param.7, bf16[8,1024,128]{2,1,0:T(8,128)(2,1)} %param.8), kind=kOutput, calls=%fused_computation.153 | convolution fusion | flops 268435456 | bytes 4718592 | tf_op jit(solution)/shard_map/htd,hte->hde/dot_general | solution.py:26
  31.0 0.0 all-gather.3.cloned.1.call-update
  31.1 4.1 %copy.92 = f32[8,1024,128]{1,2,0:T(8,128)} copy(bf16[8,1024,128]{2,1,0:T(8,128)(2,1)} %param.9) | data formatting | bytes 6291456 | tf_op jit(solution)/shard_map/convert_element_type | solution.py:29
  35.2 21.5 %fusion.107 = f32[8,1024,1024]{2,1,0:T(8,128)} fusion(bf16[8,1024,128]{2,1,0:T(8,128)(2,1)} %param.9, bf16[8,1024,128]{2,1,0:T(8,128)(2,1)} %param.8), kind=kOutput, calls=%fused_computation.154 | convolution fusion | flops 2147483648 | bytes 37748736 | tf_op jit(solution)/shard_map/htd,hsd->hts/dot_general | solution.py:50
  56.7 30.6 %multiply_reduce_fusion = (f32[1024,1024]{1,0:T(8,128)}, f32[8,1024,1024]{2,1,0:T(8,128)}) fusion(f32[8,1024,1024]{2,1,0:T(8,128)} %fusion.107, bf16[8,1024,128]{2,1,0:T(8,128)(2,1)S(1)} %copy-done, bf16[8,1024,128]{2,1,0:T(8,128)(2,1)} %param.7), kind=kOutput, calls=%fused_computation | convolution fusion | flops 2163212288 | bytes 75497472 | tf_op jit(solution)/shard_map/htd,hsd->hts/dot_general | solution.py:47
  87.3 18.2 %select_reduce_fusion.6 = (f32[1024]{0:T(1024)S(1)}, f32[1024]{0:T(1024)S(1)}, f32[1024]{0:T(1024)S(1)}, f32[1024]{0:T(1024)S(1)}, f32[1024]{0:T(1024)S(1)}, /*i...) fusion(f32[1024,1024]{1,0:T(8,128)} %get-tuple-element.44), kind=kLoop, calls=%fused_computation.43 | loop fusion | flops 81777664 | bytes 4239360 | tf_op jit(solution)/shard_map/reduce_sum | solution.py:68
  105.6 9.6 %select_multiply_fusion = f32[1024,1024]{1,0:T(8,128)S(1)} fusion(f32[1024]{0:T(1024)S(1)} %bitcast.129, f32[1024]{0:T(1024)S(1)} %bitcast.130, f32[1024]{0:T(1024)S(1)} %bitcast.131, f32[1024]{0:T(1024)S(1)} %bitcast.132, f32[1024]{0:T(1024)S(1)} %bitcast.133, f32[1024]{0:T(1024)S(1)} %bitcast.134, f32[1024]{0:T(1024)S(1)} %bitcast.135, ...), kind=kLoop, calls=%fused_computation.55 | loop fusion | flops 71303168 | bytes 4239360 | tf_op jit(solution)/shard_map/mul | solution.py:46
  115.2 0.0 copy-start.1
  115.2 18.0 %fusion.8 = f32[8,1024,128]{2,1,0:T(8,128)} fusion(bf16[8,1024,128]{2,1,0:T(8,128)(2,1)S(1)} %copy-done, f32[8,1024,1024]{2,1,0:T(8,128)} %fusion.107, f32[1024,1024]{1,0:T(8,128)S(1)} %select_multiply_fusion), kind=kOutput, calls=%fused_computation.29 | convolution fusion | flops 2164260864 | bytes 44040192 | tf_op jit(solution)/shard_map/hts,htd->hsd/dot_general | solution.py:53
  133.2 17.5 %fusion.6 = f32[8,1024,128]{2,1,0:T(8,128)} fusion(bf16[8,1024,128]{2,1,0:T(8,128)(2,1)} %param.9, f32[8,1024,1024]{2,1,0:T(8,128)} %get-tuple-element.45, f32[1024,1024]{1,0:T(8,128)S(1)} %select_multiply_fusion), kind=kOutput, calls=%fused_computation.27 | convolution fusion | flops 2164260864 | bytes 44040192 | tf_op jit(solution)/shard_map/hts,htd->hsd/dot_general | solution.py:54
  150.7 0.0 reduce-scatter.2.cloned.1.call-done
  150.8 0.0 copy-start.2
  150.8 5.1 %fusion.16 = bf16[8,1024,128]{2,1,0:T(8,128)(2,1)} fusion(f32[8,1024,128]{2,1,0:T(8,128)} %fusion.8, bf16[8,1024,128]{2,1,0:T(8,128)(2,1)} %param.8, f32[8,128,128]{1,2,0:T(8,128)} %reduce-scatter.2.cloned.1.call-done), kind=kOutput, calls=%fused_computation.39 | convolution fusion | flops 270663680 | bytes 8912896 | tf_op jit(solution)/shard_map/hte,hde->htd/dot_general | solution.py:61
  155.9 0.0 copy-done.2
  155.9 2.0 fusion.15
  158.0 62.7 %all-gather.3.cloned.1.call-done = f32[256,128,128]{2,1,0:T(8,128)} async-done(((f32[8,128,128]{2,1,0:T(8,128)}), f32[256,128,128]{2,1,0:T(8,128)}) %all-gather.3.cloned.1.call-update) | async-done | bytes 16777232 | tf_op jit(solution)/shard_map/all_gather | solution.py:101
  220.7 12.3 %select_reduce_fusion = (bf16[8,128,128]{2,1,0:T(8,128)(2,1)S(1)}, bf16[8,128,128]{2,1,0:T(8,128)(2,1)S(1)}, bf16[8,128,128]{2,1,0:T(8,128)(2,1)S(1)}, bf16[8,12...) fusion(f32[32,8,128,128]{3,2,1,0:T(8,128)} %bitcast.128, pred[32]{0:T(512)(128)(4,1)S(1)} %get-tuple-element.46, ...), kind=kLoop, calls=%fused_computation.17 | loop fusion | flops 41287680 | bytes 18088096 | tf_op jit(solution)/shard_map/reduce_sum | solution.py:106
  233.0 0.9 copy.78
  233.9 0.8 copy.77
  234.7 0.2 copy.76
  234.9 0.2 copy.75
  235.1 0.2 copy.74
  235.4 1.0 bitcast_dynamic-update-slice_fusion.1
  236.4 0.0 copy-done.6
  236.5 0.0 copy-start.9
  236.5 1.0 copy-done.9
  237.5 6.8 %multiply_reduce_fusion.1 = f32[8,128,1024]{2,1,0:T(8,128)} fusion(f32[5,1024]{1,0:T(8,128)S(1)} %slice_bitcast_fusion, bf16[5,8,128,128]{2,3,0,1:T(8,128)(2,1)S(1)} %bitcast_dynamic-update-slice_fusion, bf16[8,1024,128]{2,1,0:T(8,128)(2,1)} %param.9), kind=kOutput, calls=%fused_computation.7 | convolution fusion | flops 1351614464 | bytes 7622656 | tf_op jit(solution)/shard_map/hte,jhde->jhtd/dot_general | solution.py:59
  244.3 5.4 %copy.81 = f32[8,128,1024]{1,2,0:T(8,128)} copy(f32[8,128,1024]{2,1,0:T(8,128)} %multiply_reduce_fusion.1) | data formatting | bytes 8388608 | tf_op jit(solution)/shard_map/reduce_sum | solution.py:60
  249.7 0.0 copy-done.10
  249.7 7.2 %fusion.1 = (f32[5,1024]{1,0:T(8,128)S(1)}, f32[8,1024,128]{1,2,0:T(8,128)}) fusion(f32[8,1024,128]{1,2,0:T(8,128)} %copy.92, f32[5,1024]{1,0:T(8,128)S(1)} %slice_bitcast_fusion, bf16[5,8,128,128]{2,3,0,1:T(8,128)(2,1)S(1)} %copy-done.10, bf16[8,1024,128]{2,1,0:T(8,128)(2,1)S(1)} %copy-done), kind=kOutput, calls=%fused_computation.6 | convolution fusion | flops 1362095104 | bytes 11837440 | tf_op jit(solution)/shard_map/htd,jhde->jhte/dot_general | solution.py:57
  256.9 5.3 %copy.79 = f32[8,1024,128]{2,1,0:T(8,128)} copy(f32[8,1024,128]{1,2,0:T(8,128)} %get-tuple-element.11) | data formatting | bytes 8388608 | tf_op jit(solution)/shard_map/reduce_sum | solution.py:58
  262.2 17.4 %fusion.17 = bf16[8,1024,128]{2,1,0:T(8,128)(2,1)} fusion(f32[8,128,1024]{1,2,0:T(8,128)} %copy.81, bf16[8,1024,128]{2,1,0:T(8,128)(2,1)} %param.7, f32[8,1024,1024]{2,1,0:T(8,128)} %fusion.107, f32[1024,1024]{1,0:T(8,128)} %copy-done.1), kind=kOutput, calls=%fused_computation.41 | convolution fusion | flops 2167406592 | bytes 46137344 | tf_op jit(solution)/shard_map/hts,hsd->htd/dot_general | solution.py:52
  279.7 17.3 %add_convert_fusion = bf16[8,1024,128]{2,1,0:T(8,128)(2,1)} fusion(f32[8,1024,128]{2,1,0:T(8,128)} %copy.79, bf16[8,1024,128]{2,1,0:T(8,128)(2,1)} %param.8, f32[8,1024,1024]{2,1,0:T(8,128)} %get-tuple-element.45, f32[1024,1024]{1,0:T(8,128)} %copy-done.1), kind=kOutput, calls=%fused_computation.54 | convolution fusion | flops 2167406592 | bytes 46137344 | tf_op jit(solution)/shard_map/hts,hsd->htd/dot_general | solution.py:49
  296.9 0.1 concatenate.3
  297.0 0.5 select_reduce_fusion.5
  297.5 64.7 %psum.7 = f32[64,16]{1,0:T(8,128)S(1)} all-reduce(f32[64,16]{1,0:T(8,128)S(1)} %select_reduce_fusion.5), channel_id=1, replica_groups=mesh['ctx'=32,'heads'=4] {'ctx','heads'}, use_global_device_ids=true, to_apply=%region_23.24 | all-reduce | flops 1024 | bytes 8192 | tf_op jit(solution)/shard_map/psum | solution.py:123
  362.3 0.7 copy.93
  (27 shorter events, 0.3 us)
Async XLA Ops:
  7.2 3.9 %copy-start = (bf16[8,1024,128]{2,1,0:T(8,128)(2,1)S(1)}, bf16[8,1024,128]{2,1,0:T(8,128)(2,1)}, u32[]{:S(2)}) copy-start(bf16[8,1024,128]{2,1,0:T(8,128)(2,1)} %param.6) | copy-start | bytes 6291460
  7.2 143.6 %reduce-scatter.2.cloned.1.call-start = ((), (), s32[]{:S(2)}) async-start(), calls=%async_computation.1 | async-start | bytes 17301504 | tf_op jit(solution)/shard_map/reduce_scatter | solution.py:115
  9.0 4.8 %copy-start.3 = (bf16[8,1024,128]{2,1,0:T(8,128)(2,1)S(1)}, bf16[8,1024,128]{2,1,0:T(8,128)(2,1)}, u32[]{:S(2)}) copy-start(bf16[8,1024,128]{2,1,0:T(8,128)(2,1)} %param.9) | copy-start | bytes 6291460
  9.8 0.6 copy-start.7
  27.0 193.7 %all-gather.3.cloned.1.call-start = ((), (), s32[]{:S(2)}) async-start(), calls=%async_computation.2 | async-start | bytes 17301504 | tf_op jit(solution)/shard_map/all_gather | solution.py:101
  115.2 18.0 %copy-start.1 = (f32[1024,1024]{1,0:T(8,128)}, f32[1024,1024]{1,0:T(8,128)S(1)}, u32[]{:S(2)}) copy-start(f32[1024,1024]{1,0:T(8,128)S(1)} %select_multiply_fusion) | copy-start | bytes 12582916
  150.8 5.2 %copy-start.2 = (bf16[8,1024,128]{2,1,0:T(8,128)(2,1)S(1)}, bf16[8,1024,128]{2,1,0:T(8,128)(2,1)}, u32[]{:S(2)}) copy-start(bf16[8,1024,128]{2,1,0:T(8,128)(2,1)} %param.7) | copy-start | bytes 6291460
  150.8 5.2 %copy-start.4 = (f32[8,1024,128]{2,1,0:T(8,128)S(1)}, f32[8,1024,128]{2,1,0:T(8,128)}, u32[]{:S(2)}) copy-start(f32[8,1024,128]{2,1,0:T(8,128)} %fusion.6) | copy-start | bytes 12582916
  150.8 5.2 %copy-start.5 = (f32[8,128,128]{1,2,0:T(8,128)S(1)}, f32[8,128,128]{1,2,0:T(8,128)}, u32[]{:S(2)}) copy-start(f32[8,128,128]{1,2,0:T(8,128)} %reduce-scatter.2.cloned.1.call-done) | copy-start | bytes 1572868
  233.9 2.5 copy-start.6
  236.5 1.1 copy-start.9
  244.3 5.4 %copy-start.10 = (bf16[5,8,128,128]{2,3,0,1:T(8,128)(2,1)S(1)}, bf16[5,8,128,128]{2,3,0,1:T(8,128)(2,1)}, u32[]{:S(2)}) copy-start(bf16[5,8,128,128]{2,3,0,1:T(8,128)(2,1)} %copy-done.9) | copy-start | bytes 3932164
  279.7 17.4 %copy-start.8 = (pred[1024,64]{0,1:T(8,128)(4,1)S(1)}, pred[1024,64]{0,1:T(8,128)(4,1)}, u32[]{:S(2)}) copy-start(pred[1024,64]{0,1:T(8,128)(4,1)} %copy-done.7) | copy-start | bytes 196612
Sparse Core Ops, SparseCore 0:
  27.1 117.0 reduce-scatter.1
  147.1 73.5 all-gather.2
where the time goes:
time: 376 us; the launch traced here: 370 us
  matrix products  154 us (41%)
  blocking collectives  64.7 us (17%)
  waiting for transfers between devices  62.8 us (17%)
  other arithmetic  50.8 us (14%)
  local copies, waits for them, and re-layouts  22.4 us (6%)
  between operations  14.6 us (4%)
    psum x1, blocking collectives, body(): table_total = lax.psum(table_part, ('ctx', 'heads'))  64.7 us
    all_gather x1, waiting for transfers between devices, body(): shard_piece = lax.all_gather(states[None], 'ctx', axis=0, tiled=True)  62.7 us
    dot_general x1, matrix products, block_finish(): jnp.einsum('htd,hsd->hts', queries, keys, preferred_element_type=jnp.floa...  30.6 us
    dot_general x1, matrix products, block_finish(): jnp.einsum('htd,hsd->hts', out_grad, values, preferred_element_type=jnp.f...  21.5 us
    reduce_sum x1, other arithmetic, block_finish(): jnp.sum(jnp.where(causal & (levels == level_id), weight_grad, 0.0), 1)  18.2 us
    dot_general x1, matrix products, block_finish(): jnp.einsum('hts,htd->hsd', grad_scores, queries, preferred_element_type=j...  18 us
    dot_general x1, matrix products, block_finish(): jnp.einsum('hts,htd->hsd', weighted, out_grad, preferred_element_type=jnp...  17.5 us
    dot_general x1, matrix products, block_finish(): jnp.einsum('hts,hsd->htd', grad_scores, keys, preferred_element_type=jnp....  17.4 us
  transfers between devices with their start and end apart: 2, of which 1 were waited for; matrix products, arithmetic and copies ran while one was open for 35% of the time, Pallas kernels for 0%

commit v1 on v0

--- a/solution.py
+++ b/solution.py
@@ -98,7 +98,9 @@
     states, grads = block_start(
         queries, keys, values, out_grad, lam_tok, block_id, level_bits, factor
     )
-    shard_piece = lax.all_gather(states[None], "ctx", axis=0, tiled=True)
+    own = states[None]
+    repeated = jnp.stack([own] * lax.axis_size("ctx"))
+    shard_piece = jnp.concatenate(lax.all_to_all(repeated, "ctx", 0, 0), axis=0)
     owners = jnp.arange(shard_piece.shape[0], dtype=jnp.int32)
     pieces = []
     for bit_num in range(level_bits):

time: 376 us -> 478 us (1.27)
  waiting for transfers between devices: 62.8 us -> 111 us
  blocking collectives: 64.7 us -> 104 us
  starting transfers between devices: 0.25 us -> 8.8 us
  local copies, waits for them, and re-layouts: 22.4 us -> 29.1 us
    all_to_all x0 -> x1, waiting for transfers between devices: none -> 111 us  [body(): shard_piece = jnp.concatenate(lax.all_to_all(repeated, 'ctx', 0, 0), axis=0)]
    all_gather x1 -> x0, waiting for transfers between devices: 62.7 us -> none  [body(): shard_piece = lax.all_gather(states[None], 'ctx', axis=0, tiled=True)]
    psum x1, blocking collectives: 64.7 us -> 104 us  [body(): table_total = lax.psum(table_part, ('ctx', 'heads'))]
    all_to_all x0 -> x1, starting transfers between devices: none -> 8.76 us  [body(): shard_piece = jnp.concatenate(lax.all_to_all(repeated, 'ctx', 0, 0), axis=0)]
    another operation x0 -> x1, local copies, waits for them, and re-layouts: none -> 7.83 us  [body(): repeated = jnp.stack([own] * lax.axis_size('ctx'))]
  transfers between devices with their start and end apart: 2 -> 2, of which waited for: 1 -> 1; matrix products, arithmetic and copies ran while one was open for 35% -> 45% of each run, Pallas kernels for 0% -> 0%
where the time goes in v1:
time: 478 us; the launch traced here: 471 us
  matrix products  151 us (32%)
  waiting for transfers between devices  111 us (23%)
  blocking collectives  104 us (22%)
  other arithmetic  53.1 us (11%)
  local copies, waits for them, and re-layouts  29.1 us (6%)
  between operations  14.6 us (3%)
  starting transfers between devices  8.8 us (2%)
    all_to_all x1, waiting for transfers between devices, body(): shard_piece = jnp.concatenate(lax.all_to_all(repeated, 'ctx', 0, 0), axis=0)  111 us
    psum x1, blocking collectives, body(): table_total = lax.psum(table_part, ('ctx', 'heads'))  104 us
    dot_general x1, matrix products, block_finish(): jnp.einsum('htd,hsd->hts', queries, keys, preferred_element_type=jnp.floa...  30.4 us
    dot_general x1, matrix products, block_finish(): jnp.einsum('htd,hsd->hts', out_grad, values, preferred_element_type=jnp.f...  20.5 us
    reduce_sum x1, other arithmetic, block_finish(): jnp.sum(jnp.where(causal & (levels == level_id), weight_grad, 0.0), 1)  18.3 us
    dot_general x1, matrix products, block_finish(): jnp.einsum('hts,htd->hsd', grad_scores, queries, preferred_element_type=j...  17.7 us
    dot_general x1, matrix products, block_finish(): jnp.einsum('hts,hsd->htd', grad_scores, keys, preferred_element_type=jnp....  17.2 us
    dot_general x1, matrix products, block_finish(): jnp.einsum('hts,hsd->htd', weighted, values, preferred_element_type=jnp.f...  17.2 us
  transfers between devices with their start and end apart: 2, of which 1 were waited for; matrix products, arithmetic and copies ran while one was open for 45% of the time, Pallas kernels for 0%

profile of v1, /device:TPU:1, one launch (start us, length us, event | category | flops | bytes accessed | tf_op | source)
XLA Modules:
  0.0 471.2 jit_solution(2475311684816523685)
XLA Ops:
  7.2 0.0 copy-start
  7.2 3.1 fusion.111
  10.3 7.8 %stack.20 = f32[32,1,8,128,128]{4,3,2,1,0:T(8,128)} broadcast(f32[8,128,128]{2,1,0:T(8,128)S(1)} %fusion.111), dimensions={2,3,4} | broadcast | bytes 17301504 | tf_op jit(solution)/shard_map/stack | solution.py:102
  18.2 8.8 %all-to-all-start = ((f32[32,1,8,128,128]{4,3,2,1,0:T(8,128)}), f32[32,1,8,128,128]{4,3,2,1,0:T(8,128)}, u32[]{:S(2)}, u32[]{:S(2)}) async-start(f32[32,1,8,128,128]{4,3,2,1,0:T(8,128)} %stack.20), calls=%async_computation | async-start | bytes 33554432 | tf_op jit(solution)/shard_map/all_to_all | solution.py:103
  26.9 0.0 reduce-scatter.2.cloned.1.call-start
  27.0 0.1 broadcast_in_dim.336
  27.1 0.1 broadcast_in_dim.337
  27.2 0.1 broadcast_in_dim.331
  27.3 0.1 broadcast_in_dim.332
  27.4 0.1 broadcast_in_dim.346
  27.5 0.1 broadcast_in_dim.347
  27.6 0.1 broadcast_in_dim.341
  27.6 0.1 broadcast_in_dim.342
  27.7 0.1 broadcast_in_dim.325
  27.8 0.1 broadcast_in_dim.326
  27.9 0.1 copy.89
  28.0 0.0 copy-done.17
  28.0 0.0 copy-start.3
  28.1 0.5 select_reduce_fusion.12
  28.7 0.0 copy-done
  28.7 2.6 fusion.105
  31.3 0.0 copy-done.3
  31.4 1.1 fusion.69
  32.5 1.1 fusion.96
  33.6 1.1 fusion.87
  34.8 1.1 fusion.78
  35.9 8.9 %fusion.2 = f32[256,128,128]{1,2,0:T(8,128)} fusion(f32[8,128,128]{1,2,0:T(8,128)S(1)} %fusion.105, f32[8,128,128]{1,2,0:T(8,128)S(1)} %fusion.96, f32[8,128,128]{1,2,0:T(8,128)S(1)} %fusion.87, f32[8,128,128]{1,2,0:T(8,128)S(1)} %fusion.78, f32[8,128,128]{1,2,0:T(8,128)S(1)} %fusion.69, pred[256]{0:T(512)(128)(4,1)S(1)} %broadcast_in_dim.347, ...), kind=kLoop, calls=%fused_computation.9 | loop fusion | flops 37748736 | bytes 19399936 | tf_op jit(solution)/shard_map/add | solution.py:116
  44.8 0.0 reduce-scatter.2.cloned.1.call-update
  44.8 20.5 %fusion.112 = f32[8,1024,1024]{2,1,0:T(8,128)} fusion(bf16[8,1024,128]{2,1,0:T(8,128)(2,1)} %param.9, bf16[8,1024,128]{2,1,0:T(8,128)(2,1)} %param.8), kind=kOutput, calls=%fused_computation.159 | convolution fusion | flops 2147483648 | bytes 37748736 | tf_op jit(solution)/shard_map/htd,hsd->hts/dot_general | solution.py:50
  65.4 4.2 copy.109
  69.6 30.4 %multiply_reduce_fusion = (f32[1024,1024]{1,0:T(8,128)}, f32[8,1024,1024]{2,1,0:T(8,128)}) fusion(f32[8,1024,1024]{2,1,0:T(8,128)} %fusion.112, bf16[8,1024,128]{2,1,0:T(8,128)(2,1)S(1)} %copy-done, bf16[8,1024,128]{2,1,0:T(8,128)(2,1)} %param.7), kind=kOutput, calls=%fused_computation | convolution fusion | flops 2163212288 | bytes 75497472 | tf_op jit(solution)/shard_map/htd,hsd->hts/dot_general | solution.py:47
  100.0 18.3 %select_reduce_fusion.1 = (f32[1024]{0:T(1024)S(1)}, f32[1024]{0:T(1024)S(1)}, f32[1024]{0:T(1024)S(1)}, f32[1024]{0:T(1024)S(1)}, f32[1024]{0:T(1024)S(1)}, /*i...) fusion(f32[1024,1024]{1,0:T(8,128)} %get-tuple-element.44), kind=kLoop, calls=%fused_computation.48 | loop fusion | flops 81777664 | bytes 4239360 | tf_op jit(solution)/shard_map/reduce_sum | solution.py:68
  118.4 0.6 broadcast_multiply_fusion.3
  119.0 0.6 broadcast_multiply_fusion.5
  119.6 0.6 broadcast_multiply_fusion.7
  120.2 0.6 broadcast_multiply_fusion.9
  120.8 9.6 %select_multiply_fusion = f32[1024,1024]{1,0:T(8,128)S(1)} fusion(f32[1024]{0:T(1024)S(1)} %bitcast.143, f32[1024]{0:T(1024)S(1)} %bitcast.144, f32[1024]{0:T(1024)S(1)} %bitcast.145, f32[1024]{0:T(1024)S(1)} %bitcast.146, f32[1024]{0:T(1024)S(1)} %bitcast.147, f32[1024]{0:T(1024)S(1)} %bitcast.148, f32[1024]{0:T(1024)S(1)} %bitcast.149, ...), kind=kLoop, calls=%fused_computation.60 | loop fusion | flops 71303168 | bytes 4239360 | tf_op jit(solution)/shard_map/mul | solution.py:46
  130.4 17.7 %fusion.13 = f32[8,1024,128]{2,1,0:T(8,128)} fusion(bf16[8,1024,128]{2,1,0:T(8,128)(2,1)S(1)} %copy-done, f32[8,1024,1024]{2,1,0:T(8,128)} %fusion.112, f32[1024,1024]{1,0:T(8,128)S(1)} %select_multiply_fusion), kind=kOutput, calls=%fused_computation.34 | convolution fusion | flops 2164260864 | bytes 44040192 | tf_op jit(solution)/shard_map/hts,htd->hsd/dot_general | solution.py:53
  148.1 16.7 %fusion.11 = f32[8,1024,128]{2,1,0:T(8,128)} fusion(bf16[8,1024,128]{2,1,0:T(8,128)(2,1)} %param.9, f32[8,1024,1024]{2,1,0:T(8,128)} %get-tuple-element.45, f32[1024,1024]{1,0:T(8,128)S(1)} %select_multiply_fusion), kind=kOutput, calls=%fused_computation.32 | convolution fusion | flops 2164260864 | bytes 44040192 | tf_op jit(solution)/shard_map/hts,htd->hsd/dot_general | solution.py:54
  164.8 110.7 %all-to-all-done = f32[32,1,8,128,128]{4,3,2,1,0:T(8,128)} async-done(((f32[32,1,8,128,128]{4,3,2,1,0:T(8,128)}), f32[32,1,8,128,128]{4,3,2,1,0:T(8,128)}, u32[]{:S(2)}, u32[]{:S(2)}) %all-to-all-start) | async-done | bytes 16777248 | tf_op jit(solution)/shard_map/all_to_all | solution.py:103
  275.5 12.7 %fusion.10 = (bf16[8,128,128]{2,1,0:T(8,128)(2,1)S(1)}, bf16[8,128,128]{2,1,0:T(8,128)(2,1)S(1)}, bf16[8,128,128]{2,1,0:T(8,128)(2,1)S(1)}, bf16[8,128,128]{2,1,0:T(8,128)(2,1)S(1)}, bf16[8,128,128]{2,1,0:T(8,128)(2,1)S(1)}) fusion(f32[32,1,8,128,128]{4,3,2,1,0:T(8,128)} %all-to-all-done, pred[32]{0:T(512)(128)(4,1)S(1)} %get-tuple-element.46, ...), kind=kLoop, calls=%fused_computation.26 | loop fusion | flops 41287680 | bytes 18088096 | tf_op jit(solution)/shard_map/reduce_sum | solution.py:108
  288.2 0.9 copy.95
  289.1 0.8 copy.92
  289.9 0.2 copy.93
  290.1 0.2 copy.94
  290.3 0.2 copy.91
  290.5 1.0 bitcast_dynamic-update-slice_fusion.3
  291.6 0.0 copy-start.7
  291.6 1.0 copy-done.7
  292.7 6.8 %multiply_reduce_fusion.1 = f32[8,128,1024]{2,1,0:T(8,128)} fusion(f32[5,1024]{1,0:T(8,128)S(1)} %slice_bitcast_fusion, bf16[5,8,128,128]{2,3,0,1:T(8,128)(2,1)S(1)} %bitcast_dynamic-update-slice_fusion, bf16[8,1024,128]{2,1,0:T(8,128)(2,1)} %param.9), kind=kOutput, calls=%fused_computation.7 | convolution fusion | flops 1351614464 | bytes 7622656 | tf_op jit(solution)/shard_map/hte,jhde->jhtd/dot_general | solution.py:59
  299.5 5.4 %copy.98 = f32[8,128,1024]{1,2,0:T(8,128)} copy(f32[8,128,1024]{2,1,0:T(8,128)} %multiply_reduce_fusion.1) | data formatting | bytes 8388608 | tf_op jit(solution)/shard_map/reduce_sum | solution.py:60
  304.9 7.2 %fusion.1 = (f32[5,1024]{1,0:T(8,128)S(1)}, f32[8,1024,128]{1,2,0:T(8,128)}) fusion(f32[8,1024,128]{1,2,0:T(8,128)} %copy.109, f32[5,1024]{1,0:T(8,128)S(1)} %slice_bitcast_fusion, bf16[5,8,128,128]{2,3,0,1:T(8,128)(2,1)S(1)} %copy-done.8, bf16[8,1024,128]{2,1,0:T(8,128)(2,1)S(1)} %copy-done), kind=kOutput, calls=%fused_computation.6 | convolution fusion | flops 1362095104 | bytes 11837440 | tf_op jit(solution)/shard_map/htd,jhde->jhte/dot_general | solution.py:57
  312.1 0.0 copy-start.14
  312.2 0.0 copy-start.15
  312.2 5.3 %copy.96 = f32[8,1024,128]{2,1,0:T(8,128)} copy(f32[8,1024,128]{1,2,0:T(8,128)} %get-tuple-element.11) | data formatting | bytes 8388608 | tf_op jit(solution)/shard_map/reduce_sum | solution.py:58
  317.5 0.0 copy-done.9
  317.6 0.1 concatenate.3
  317.7 0.5 select_reduce_fusion
  318.2 103.6 %psum.7 = f32[64,16]{1,0:T(8,128)S(1)} all-reduce(f32[64,16]{1,0:T(8,128)S(1)} %select_reduce_fusion), channel_id=1, replica_groups=mesh['ctx'=32,'heads'=4] {'ctx','heads'}, use_global_device_ids=true, to_apply=%region_23.24 | all-reduce | flops 1024 | bytes 8192 | tf_op jit(solution)/shard_map/psum | solution.py:125
  421.8 0.7 copy.110
  422.5 17.2 %fusion.22 = bf16[8,1024,128]{2,1,0:T(8,128)(2,1)} fusion(f32[8,128,1024]{1,2,0:T(8,128)} %copy.98, bf16[8,1024,128]{2,1,0:T(8,128)(2,1)} %param.7, f32[8,1024,1024]{2,1,0:T(8,128)} %fusion.112, f32[1024,1024]{1,0:T(8,128)} %copy-done.1), kind=kOutput, calls=%fused_computation.46 | convolution fusion | flops 2167406592 | bytes 46137344 | tf_op jit(solution)/shard_map/hts,hsd->htd/dot_general | solution.py:52
  439.7 17.2 %add_convert_fusion = bf16[8,1024,128]{2,1,0:T(8,128)(2,1)} fusion(f32[8,1024,128]{2,1,0:T(8,128)} %copy.96, bf16[8,1024,128]{2,1,0:T(8,128)(2,1)} %param.8, f32[8,1024,1024]{2,1,0:T(8,128)} %get-tuple-element.45, f32[1024,1024]{1,0:T(8,128)} %copy-done.1), kind=kOutput, calls=%fused_computation.59 | convolution fusion | flops 2167406592 | bytes 46137344 | tf_op jit(solution)/shard_map/hts,hsd->htd/dot_general | solution.py:49
  457.0 5.1 %fusion.21 = bf16[8,1024,128]{2,1,0:T(8,128)(2,1)} fusion(f32[8,1024,128]{2,1,0:T(8,128)} %fusion.13, bf16[8,1024,128]{2,1,0:T(8,128)(2,1)} %param.8, f32[8,128,128]{1,2,0:T(8,128)} %reduce-scatter.2.cloned.1.call-done), kind=kOutput, calls=%fused_computation.44 | convolution fusion | flops 270663680 | bytes 8912896 | tf_op jit(solution)/shard_map/hte,hde->htd/dot_general | solution.py:61
  462.1 2.0 fusion.20
  (41 shorter events, 0.3 us)
Async XLA Ops:
  7.2 21.5 %copy-start = (bf16[8,1024,128]{2,1,0:T(8,128)(2,1)S(1)}, bf16[8,1024,128]{2,1,0:T(8,128)(2,1)}, u32[]{:S(2)}) copy-start(bf16[8,1024,128]{2,1,0:T(8,128)(2,1)} %param.6) | copy-start | bytes 6291460
  18.1 9.8 %copy-start.16 = (f32[64,16]{0,1:T(8,128)S(1)}, f32[64,16]{0,1:T(8,128)}, u32[]{:S(2)}) copy-start(f32[64,16]{0,1:T(8,128)} %param.10) | copy-start | bytes 12292
  18.1 9.9 %copy-start.17 = (s32[1024]{0:T(1024)S(1)}, s32[1024]{0:T(1024)}, u32[]{:S(2)}) copy-start(s32[1024]{0:T(1024)} %param.11) | copy-start | bytes 12292
  18.2 257.3 %all-to-all-start = ((f32[32,1,8,128,128]{4,3,2,1,0:T(8,128)}), f32[32,1,8,128,128]{4,3,2,1,0:T(8,128)}, u32[]{:S(2)}, u32[]{:S(2)}) async-start(f32[32,1,8,128,128]{4,3,2,1,0:T(8,128)} %stack.20), calls=%async_computation | async-start | bytes 33554432 | tf_op jit(solution)/shard_map/all_to_all | solution.py:103
  26.9 430.0 %reduce-scatter.2.cloned.1.call-start = ((), (), s32[]{:S(2)}) async-start(), calls=%async_computation.2 | async-start | bytes 17301504 | tf_op jit(solution)/shard_map/reduce_scatter | solution.py:117
  28.0 3.3 copy-start.3
  130.4 17.7 %copy-start.1 = (f32[1024,1024]{1,0:T(8,128)}, f32[1024,1024]{1,0:T(8,128)S(1)}, u32[]{:S(2)}) copy-start(f32[1024,1024]{1,0:T(8,128)S(1)} %select_multiply_fusion) | copy-start | bytes 12582916
  289.1 2.5 copy-start.6
  291.6 1.1 copy-start.7
  299.5 5.4 %copy-start.8 = (bf16[5,8,128,128]{2,3,0,1:T(8,128)(2,1)S(1)}, bf16[5,8,128,128]{2,3,0,1:T(8,128)(2,1)}, u32[]{:S(2)}) copy-start(bf16[5,8,128,128]{2,3,0,1:T(8,128)(2,1)} %copy-done.7) | copy-start | bytes 3932164
  312.1 5.4 %copy-start.9 = (f32[1024]{0:T(1024)S(1)}, f32[1024]{0:T(1024)}, u32[]{:S(2)}) copy-start(f32[1024]{0:T(1024)} %get-tuple-element.53) | copy-start | bytes 12292
  312.1 5.4 %copy-start.10 = (f32[1024]{0:T(1024)S(1)}, f32[1024]{0:T(1024)}, u32[]{:S(2)}) copy-start(f32[1024]{0:T(1024)} %get-tuple-element.54) | copy-start | bytes 12292
  312.1 5.4 %copy-start.11 = (f32[1024]{0:T(1024)S(1)}, f32[1024]{0:T(1024)}, u32[]{:S(2)}) copy-start(f32[1024]{0:T(1024)} %get-tuple-element.55) | copy-start | bytes 12292
  312.1 5.4 %copy-start.12 = (f32[1024]{0:T(1024)S(1)}, f32[1024]{0:T(1024)}, u32[]{:S(2)}) copy-start(f32[1024]{0:T(1024)} %get-tuple-element.56) | copy-start | bytes 12292
  312.1 5.4 %copy-start.13 = (f32[1024]{0:T(1024)S(1)}, f32[1024]{0:T(1024)}, u32[]{:S(2)}) copy-start(f32[1024]{0:T(1024)} %get-tuple-element.57) | copy-start | bytes 12292
  312.1 5.4 %copy-start.14 = (f32[1024]{0:T(1024)S(1)}, f32[1024]{0:T(1024)}, u32[]{:S(2)}) copy-start(f32[1024]{0:T(1024)} %get-tuple-element.58) | copy-start | bytes 12292
  312.2 5.4 %copy-start.15 = (f32[1024]{0:T(1024)S(1)}, f32[1024]{0:T(1024)}, u32[]{:S(2)}) copy-start(f32[1024]{0:T(1024)} %get-tuple-element.59) | copy-start | bytes 12292
  457.0 5.2 %copy-start.2 = (bf16[8,1024,128]{2,1,0:T(8,128)(2,1)S(1)}, bf16[8,1024,128]{2,1,0:T(8,128)(2,1)}, u32[]{:S(2)}) copy-start(bf16[8,1024,128]{2,1,0:T(8,128)(2,1)} %param.7) | copy-start | bytes 6291460
  457.0 5.2 %copy-start.4 = (f32[8,1024,128]{2,1,0:T(8,128)S(1)}, f32[8,1024,128]{2,1,0:T(8,128)}, u32[]{:S(2)}) copy-start(f32[8,1024,128]{2,1,0:T(8,128)} %fusion.11) | copy-start | bytes 12582916
  457.0 5.2 %copy-start.5 = (f32[8,128,128]{1,2,0:T(8,128)S(1)}, f32[8,128,128]{1,2,0:T(8,128)}, u32[]{:S(2)}) copy-start(f32[8,128,128]{1,2,0:T(8,128)} %reduce-scatter.2.cloned.1.call-done) | copy-start | bytes 1572868
Sparse Core Ops, SparseCore 0:
  45.0 257.7 reduce-scatter.1
